TPU v7x, 128 devices: a whole 4x4x4 slice. The times are simulated.
128 devices in a mesh: slab: 16 (over x, y_hi, core), tile: 8 (over y_lo, z).
Axes of the slice: x: 4, y: 4 (y_hi: 2, y_lo: 2; y = y_hi * 2 + y_lo), z: 4, core: 2. Of those that a mesh axis runs over, the one named last changes fastest.
Arguments:
- velocity: float32 [3, 512, 128, 128], P(None, 'slab', 'tile'), may hold values from -4 to 4
- viscosity: float32 [512, 128, 128], P('slab', 'tile'), may hold values from 0.2 to 0.6
- basis: bfloat16 [32, 3, 512, 128, 128], P(None, None, ('slab', 'tile')), may hold values from -6 to 6
- sigma: float32 [32], replicated, may hold values from 0.3 to 3
- rotation: float32 [35, 32], replicated, may hold values from -1 to 1
Outputs:
- advanced: float32 [3, 512, 128, 128], P(None, 'slab', 'tile')
- r_factor: float32 [35, 35], replicated
- new_basis: bfloat16 [32, 3, 512, 128, 128], P(None, None, ('slab', 'tile'))
All inputs are finite; a program needn't handle non-finite values.
Results may differ from a plain program's by a relative error of at most 0.001.
Values sent between devices are 32-bit elements; how exact they have to be, the bound alone decides.
A program may use at most 256 MiB of HBM per device.

v0:
```python
import math
import jax
import jax.numpy as jnp
from jax import lax
from jax.sharding import PartitionSpec as P

step_size = 0.25


def extended(block, sides, width):
    for axis, dim in sides:
        count = lax.axis_size(axis)
        forward = [(i, i + 1) for i in range(count - 1)]
        forward.append((count - 1, 0))
        backward = [(target, source) for source, target in forward]
        low = lax.ppermute(
            lax.slice_in_dim(block, block.shape[dim] - width, None, axis=dim), axis, forward
        )
        high = lax.ppermute(lax.slice_in_dim(block, 0, width, axis=dim), axis, backward)
        block = jnp.concatenate([low, block, high], axis=dim)
    return block


def upper_factor(gram):
    order = gram.shape[0]
    positions = jnp.arange(order)
    factor = jnp.zeros_like(gram)
    for column_index in range(order):
        above = factor[:, column_index]
        remainder = gram[column_index] - jnp.dot(
            above, factor, precision=lax.Precision.HIGHEST, preferred_element_type=jnp.float32
        )
        pivot = jnp.sqrt(remainder[column_index])
        new_row = jnp.where(positions >= column_index, remainder / pivot, 0.0)
        factor = factor.at[column_index].set(new_row)
    return factor


def upper_solve(factor, right_hand):
    order = factor.shape[0]
    solved = jnp.zeros_like(right_hand)
    for row_index in range(order - 1, -1, -1):
        partial_sum = jnp.dot(
            factor[row_index],
            solved,
            precision=lax.Precision.HIGHEST,
            preferred_element_type=jnp.float32,
        )
        solved = solved.at[row_index].set(
            (right_hand[row_index] - partial_sum) / factor[row_index, row_index]
        )
    return solved


def advance(padded, viscosity):
    centre = padded[:, 1:-1, 1:-1, :]
    forward_x = padded[:, 2:, 1:-1, :]
    backward_x = padded[:, :-2, 1:-1, :]
    forward_z = padded[:, 1:-1, 2:, :]
    backward_z = padded[:, 1:-1, :-2, :]
    walled = jnp.pad(centre, ((0, 0), (0, 0), (0, 0), (1, 1)))
    above_y = walled[..., 2:]
    below_y = walled[..., :-2]
    laplace = forward_x + backward_x + forward_z + backward_z + above_y + below_y - 6.0 * centre
    carried = (
        centre[0:1] * (forward_x - backward_x)
        + centre[1:2] * (above_y - below_y)
        + centre[2:3] * (forward_z - backward_z)
    )
    return centre + step_size * (viscosity * laplace - 0.5 * carried)


def shards(velocity, viscosity, basis, sigma, rotation):
    current = velocity
    history = [velocity]
    for repeat in range(2):
        padded = extended(current, (("slab", 1), ("tile", 2)), 1)
        current = advance(padded, viscosity)
        history.append(current)
    snapshots = lax.all_to_all(jnp.stack(history), "tile", split_axis=2, concat_axis=3, tiled=True)
    strip_width = basis.shape[2]
    row_count = (
        3
        * strip_width
        * lax.axis_size("slab")
        * lax.axis_size("tile")
        * basis.shape[3]
        * basis.shape[4]
    )
    row_scale = math.sqrt(row_count)
    width_all = sigma.shape[0] + 3
    scaled = basis.astype(jnp.float32) * sigma[:, None, None, None, None]
    columns = jnp.concatenate([scaled, snapshots], 0).reshape(width_all, -1)
    local_gram = jnp.dot(
        columns, columns.T, precision=lax.Precision.HIGHEST, preferred_element_type=jnp.float32
    )
    gram = lax.psum(local_gram, ("slab", "tile"))
    factor = upper_factor(gram)
    mixing = upper_solve(factor, rotation) * row_scale
    rotated = jnp.dot(
        mixing.T, columns, precision=lax.Precision.HIGHEST, preferred_element_type=jnp.float32
    )
    rotated = rotated.reshape(basis.shape).astype(jnp.bfloat16)
    return (current, factor / row_scale, rotated)


def solution(mesh):
    in_specs = (
        P(None, "slab", "tile", None),
        P("slab", "tile", None),
        P(None, None, ("slab", "tile"), None, None),
        P(),
        P(),
    )
    out_specs = (P(None, "slab", "tile", None), P(), P(None, None, ("slab", "tile"), None, None))
    return jax.shard_map(shards, mesh=mesh, in_specs=in_specs, out_specs=out_specs, check_vma=False)
```

profile of v0, /device:TPU:1, one launch (start us, length us, event | category | flops | bytes accessed | tf_op | source)
XLA Modules:
  0.0 461.0 jit_solution(1416673244914366114)
XLA Ops:
  1.4 4.3 collective-permute-start.1
  6.7 1.2 copy_bitcast_fusion.1
  7.9 2.6 collective-permute-done
  10.5 3.9 collective-permute-start.2
  14.5 1.2 slice_bitcast_fusion.5
  15.6 1.2 copy.42
  16.8 2.7 collective-permute-done.3
  19.6 1.8 multiply_add_fusion.1
  21.4 3.4 collective-permute-start.5
  25.7 4.1 collective-permute-done.4
  30.0 1.5 collective-permute-start.7
  31.5 1.4 collective-permute-done.6
  32.9 2.2 collective-permute-done.7
  35.1 1.8 fusion.306
  36.9 1.6 pad_maximum_fusion.1
  38.6 3.8 all-to-all-start
  42.4 11.8 %convert_multiply_fusion = f32[32,3,4,128,128]{4,0,3,2,1:T(8,128)S(1)} fusion(bf16[32,3,4,128,128]{4,3,2,1,0:T(8,128)(2,1)} %param.147, f32[32]{0:T(128)} %param.148), kind=kLoop, calls=%fused_computation.8 | loop fusion | flops 12582912 | bytes 37748864 | tf_op jit(solution)/shard_map/mul | solution.py:92
  54.1 28.1 %copy.82 = f32[32,3,4,128,128]{4,3,2,1,0:T(8,128)} copy(f32[32,3,4,128,128]{4,0,3,2,1:T(8,128)S(1)} %convert_multiply_fusion) | data formatting | bytes 50331648 | tf_op jit(solution)/shard_map/mul | solution.py:92
  82.3 25.1 %copy.100 = f32[4,8,1536,128]{3,1,2,0:T(8,128)} copy(f32[4,8,1536,128]{3,2,1,0:T(8,128)} %bitcast.1128) | data formatting | bytes 50331648
  107.4 1.0 slice_reduce_fusion.35
  108.5 1.1 slice_reduce_fusion.34
  110.7 0.9 copy.84
  111.6 1.4 copy-done.3
  113.0 3.0 copy.46
  116.0 28.8 %fusion.9 = f32[35,35]{1,0:T(8,128)S(1)} fusion(f32[3,3,4,128,128]{4,0,3,2,1:T(4,128)S(1)} %bitcast.1130, f32[32,3,4,128,128]{4,0,3,2,1:T(8,128)} %copy-done.1), kind=kOutput, calls=%fused_computation.15 | convolution fusion | flops 2897018880 | bytes 27530020 | tf_op jit(solution)/shard_map/dot_general | solution.py:94
  144.8 68.9 %psum.7 = f32[35,35]{1,0:T(8,128)S(1)} all-reduce(f32[35,35]{1,0:T(8,128)S(1)} %fusion.9), channel_id=1, replica_groups=mesh['slab'=16,'tile'=8] {'slab','tile'}, use_global_device_ids=true, to_apply=%region_0.1 | all-reduce | flops 1225 | bytes 9800 | tf_op jit(solution)/shard_map/psum | solution.py:97
  298.0 1.4 fusion.87
  299.7 1.5 fusion.89
  301.4 1.4 fusion.91
  303.0 1.4 fusion.93
  304.7 1.4 fusion.95
  306.4 1.4 fusion.97
  308.1 1.5 fusion.99
  309.9 1.4 fusion.101
  311.6 1.4 fusion.103
  313.2 1.5 fusion.105
  315.0 1.4 fusion.107
  316.6 1.5 fusion.109
  318.3 1.4 fusion.111
  320.0 1.4 fusion.113
  321.7 1.4 fusion.115
  323.3 1.5 fusion.117
  325.1 1.4 fusion.119
  326.7 1.4 fusion.121
  328.4 1.4 fusion.123
  330.0 1.4 fusion.125
  331.7 1.5 fusion.127
  333.4 1.5 fusion.129
  335.2 1.4 fusion.131
  336.8 1.5 fusion.133
  338.6 1.4 fusion.135
  340.3 1.4 fusion.137
  342.0 1.4 fusion.139
  343.7 1.4 fusion.141
  345.3 1.5 fusion.143
  347.0 1.4 fusion.145
  348.6 1.4 fusion.147
  350.3 1.4 fusion.149
  352.0 1.4 fusion.151
  353.6 10.1 %pad_maximum_fusion = f32[35,196608]{1,0:T(8,128)S(1)} fusion(f32[3,196608]{1,0:T(4,128)S(1)} %bitcast.1131, f32[32,196608]{1,0:T(8,128)} %bitcast.1127), kind=kLoop, calls=%fused_computation.4 | loop fusion | flops 6881280 | bytes 55050240 | tf_op jit(solution)/shard_map/concatenate | solution.py:93
  363.7 14.4 %copy.89 = f32[5,8,1536,128]{3,2,1,0:T(8,128)} copy(f32[5,8,1536,128]{3,1,2,0:T(8,128)S(1)} %bitcast.1125) | data formatting | bytes 62914560
  378.1 20.3 %slice.2142 = f32[35,1536,128]{2,1,0:T(8,128)} slice(f32[40,1536,128]{2,1,0:T(8,128)} %bitcast.1126), slice={[0:35], [0:1536], [0:128]} | slice | bytes 55050240
  398.3 48.0 %fusion.6 = bf16[32,3,4,128,128]{4,0,3,2,1:T(8,128)(2,1)S(1)} fusion(f32[3,4,128,128,35]{3,2,1,0,4:T(8,128)} %bitcast.1124, f32[35,32]{0,1:T(8,128)S(1)} %scatter.349), kind=kOutput, calls=%fused_computation.9 | convolution fusion | flops 2648704000 | bytes 40112512 | tf_op jit(solution)/shard_map/dot_general | solution.py:100
  446.4 14.5 %copy.85 = bf16[32,3,4,128,128]{4,3,2,1,0:T(8,128)(2,1)} copy(bf16[32,3,4,128,128]{4,0,3,2,1:T(8,128)(2,1)S(1)} %fusion.6) | data formatting | bytes 25165824
  (336 shorter events, 71.9 us)
Async XLA Ops:
  1.4 5.3 %collective-permute-start.1 = (f32[3,1,16,128]{3,2,0,1:T(8,128)S(1)}, f32[3,1,16,128]{3,2,0,1:T(8,128)S(1)}, u32[]{:S(2)}, u32[]{:S(2)}) collective-permute-start(f32[3,1,16,128]{3,2,0,1:T(8,128)S(1)} %get-tuple-element.905), channel_id=1, source_target_pairs={{0,8},{8,16},{16,24},{24,32},{32,40},{40,48},{48,56},{56,64},{64,7... | collective-permute-start | bytes 73736 | tf_op jit(solution)/shard_map/ppermute | solution.py:16
  5.7 4.8 %collective-permute-start = (f32[3,1,16,128]{3,2,0,1:T(8,128)S(1)}, f32[3,1,16,128]{3,2,0,1:T(8,128)S(1)}, u32[]{:S(2)}, u32[]{:S(2)}) collective-permute-start(f32[3,1,16,128]{3,2,0,1:T(8,128)S(1)} %get-tuple-element.904), channel_id=1, source_target_pairs={{8,0},{16,8},{24,16},{32,24},{40,32},{48,40},{56,48},{64,56},{72,6... | collective-permute-start | bytes 73736 | tf_op jit(solution)/shard_map/ppermute | solution.py:19
  10.5 6.3 %collective-permute-start.2 = (f32[3,34,1,128]{3,2,0,1:T(1,128)S(1)}, f32[3,34,1,128]{3,2,0,1:T(1,128)S(1)}, u32[]{:S(2)}, u32[]{:S(2)}) collective-permute-start(f32[3,34,1,128]{3,2,0,1:T(1,128)S(1)} %get-tuple-element.892), channel_id=1, source_target_pairs={{1,0},{2,1},{3,2},{4,3},{5,4},{6,5},{7,6},{0,7},{9,8},{10,9},{11,1... | collective-permute-start | bytes 156680 | tf_op jit(solution)/shard_map/ppermute | solution.py:19
  14.5 5.1 %collective-permute-start.3 = (f32[3,34,1,128]{3,2,0,1:T(1,128)S(1)}, f32[3,34,1,128]{3,2,0,1:T(1,128)S(1)}, u32[]{:S(2)}, u32[]{:S(2)}) collective-permute-start(f32[3,34,1,128]{3,2,0,1:T(1,128)S(1)} %get-tuple-element.893), channel_id=1, source_target_pairs={{0,1},{1,2},{2,3},{3,4},{4,5},{5,6},{6,7},{7,0},{8,9},{9,10},{10,1... | collective-permute-start | bytes 156680 | tf_op jit(solution)/shard_map/ppermute | solution.py:16
  21.4 4.3 collective-permute-start.5
  24.8 5.1 %collective-permute-start.4 = (f32[3,1,16,128]{3,2,0,1:T(8,128)S(1)}, f32[3,1,16,128]{3,2,0,1:T(8,128)S(1)}, u32[]{:S(2)}, u32[]{:S(2)}) collective-permute-start(f32[3,1,16,128]{3,2,0,1:T(8,128)S(1)} %get-tuple-element.900), channel_id=1, source_target_pairs={{8,0},{16,8},{24,16},{32,24},{40,32},{48,40},{56,48},{64,56},{72,6... | collective-permute-start | bytes 73736 | tf_op jit(solution)/shard_map/ppermute | solution.py:19
  29.9 3.0 collective-permute-start.6
  30.0 5.2 %collective-permute-start.7 = (f32[3,34,1,128]{3,2,0,1:T(1,128)S(1)}, f32[3,34,1,128]{3,2,0,1:T(1,128)S(1)}, u32[]{:S(2)}, u32[]{:S(2)}) collective-permute-start(f32[3,34,1,128]{3,2,0,1:T(1,128)S(1)} %get-tuple-element.891), channel_id=1, source_target_pairs={{0,1},{1,2},{2,3},{3,4},{4,5},{5,6},{6,7},{7,0},{8,9},{9,10},{10,1... | collective-permute-start | bytes 156680 | tf_op jit(solution)/shard_map/ppermute | solution.py:16
  31.5 7.0 %copy-start.4 = (f32[32,16,128]{2,1,0:T(8,128)}, f32[32,16,128]{2,1,0:T(8,128)S(1)}, u32[]{:S(2)}) copy-start(f32[32,16,128]{2,1,0:T(8,128)S(1)} %get-tuple-element.897) | copy-start | bytes 786436
  31.5 7.0 %copy-start.6 = (f32[32,16,128]{2,1,0:T(8,128)}, f32[32,16,128]{2,1,0:T(8,128)S(1)}, u32[]{:S(2)}) copy-start(f32[32,16,128]{2,1,0:T(8,128)S(1)} %get-tuple-element.898) | copy-start | bytes 786436
  35.1 3.4 copy-start.10
  38.6 73.0 %all-to-all-start = ((f32[3,3,32,16,128]{4,3,1,0,2:T(8,128)}), f32[3,3,32,16,128]{4,3,1,0,2:T(8,128)S(1)}, u32[]{:S(2)}, u32[]{:S(2)}) async-start(f32[3,3,32,16,128]{4,3,1,0,2:T(8,128)} %pad_maximum_fusion.1), calls=%async_computation | async-start | bytes 4718592 | tf_op jit(solution)/shard_map/all_to_all | solution.py:80
  54.1 28.2 %copy-start.1 = (f32[32,3,4,128,128]{4,0,3,2,1:T(8,128)}, f32[32,3,4,128,128]{4,0,3,2,1:T(8,128)S(1)}, u32[]{:S(2)}) copy-start(f32[32,3,4,128,128]{4,0,3,2,1:T(8,128)S(1)} %convert_multiply_fusion) | copy-start | bytes 75497472
  82.3 25.1 %copy-start.2 = (f32[35,32]{0,1:T(8,128)S(1)}, f32[35,32]{0,1:T(8,128)}, u32[]{:S(2)}) copy-start(f32[35,32]{0,1:T(8,128)} %param.149) | copy-start | bytes 13444
  82.3 27.3 %copy-start.5 = (f32[32,16,128]{2,1,0:T(8,128)S(1)}, f32[32,16,128]{2,1,0:T(8,128)}, u32[]{:S(2)}) copy-start(f32[32,16,128]{2,1,0:T(8,128)} %copy-done.4) | copy-start | bytes 786436
  82.3 27.3 %copy-start.7 = (f32[32,16,128]{2,1,0:T(8,128)S(1)}, f32[32,16,128]{2,1,0:T(8,128)}, u32[]{:S(2)}) copy-start(f32[32,16,128]{2,1,0:T(8,128)} %copy-done.6) | copy-start | bytes 786436
  82.3 27.2 %copy-start.8 = (f32[32,16,128]{2,1,0:T(8,128)S(1)}, f32[32,16,128]{2,1,0:T(8,128)}, u32[]{:S(2)}) copy-start(f32[32,16,128]{2,1,0:T(8,128)} %param.146) | copy-start | bytes 786436
  82.3 27.2 %copy-start.11 = (f32[3,34,1,128]{3,2,0,1:T(1,128)S(1)}, f32[3,34,1,128]{3,2,0,1:T(1,128)}, u32[]{:S(2)}) copy-start(f32[3,34,1,128]{3,2,0,1:T(1,128)} %copy-done.10) | copy-start | bytes 156676
  110.4 185.6 %copy-start.35 = (f32[32]{0:T(128)S(1)}, f32[32]{0:T(128)}, u32[]{:S(2)}) copy-start(f32[32]{0:T(128)} %get-tuple-element.889) | copy-start | bytes 388
  110.4 186.4 %copy-start.30 = (f32[32]{0:T(128)S(1)}, f32[32]{0:T(128)}, u32[]{:S(2)}) copy-start(f32[32]{0:T(128)} %get-tuple-element.888) | copy-start | bytes 388
  110.4 187.5 %copy-start.29 = (f32[32]{0:T(128)S(1)}, f32[32]{0:T(128)}, u32[]{:S(2)}) copy-start(f32[32]{0:T(128)} %get-tuple-element.887) | copy-start | bytes 388
  110.4 189.2 %copy-start.34 = (f32[32]{0:T(128)S(1)}, f32[32]{0:T(128)}, u32[]{:S(2)}) copy-start(f32[32]{0:T(128)} %get-tuple-element.886) | copy-start | bytes 388
  110.5 191.0 %copy-start.28 = (f32[32]{0:T(128)S(1)}, f32[32]{0:T(128)}, u32[]{:S(2)}) copy-start(f32[32]{0:T(128)} %get-tuple-element.885) | copy-start | bytes 388
  110.5 192.6 %copy-start.27 = (f32[32]{0:T(128)S(1)}, f32[32]{0:T(128)}, u32[]{:S(2)}) copy-start(f32[32]{0:T(128)} %get-tuple-element.884) | copy-start | bytes 388
  110.5 194.3 %copy-start.26 = (f32[32]{0:T(128)S(1)}, f32[32]{0:T(128)}, u32[]{:S(2)}) copy-start(f32[32]{0:T(128)} %get-tuple-element.883) | copy-start | bytes 388
  110.5 196.0 %copy-start.25 = (f32[32]{0:T(128)S(1)}, f32[32]{0:T(128)}, u32[]{:S(2)}) copy-start(f32[32]{0:T(128)} %get-tuple-element.882) | copy-start | bytes 388
  110.5 197.6 %copy-start.24 = (f32[32]{0:T(128)S(1)}, f32[32]{0:T(128)}, u32[]{:S(2)}) copy-start(f32[32]{0:T(128)} %get-tuple-element.881) | copy-start | bytes 388
  110.5 199.4 %copy-start.23 = (f32[32]{0:T(128)S(1)}, f32[32]{0:T(128)}, u32[]{:S(2)}) copy-start(f32[32]{0:T(128)} %get-tuple-element.880) | copy-start | bytes 388
  110.5 201.1 %copy-start.22 = (f32[32]{0:T(128)S(1)}, f32[32]{0:T(128)}, u32[]{:S(2)}) copy-start(f32[32]{0:T(128)} %get-tuple-element.879) | copy-start | bytes 388
  110.5 202.7 %copy-start.33 = (f32[32]{0:T(128)S(1)}, f32[32]{0:T(128)}, u32[]{:S(2)}) copy-start(f32[32]{0:T(128)} %get-tuple-element.878) | copy-start | bytes 388
  110.5 204.4 %copy-start.21 = (f32[32]{0:T(128)S(1)}, f32[32]{0:T(128)}, u32[]{:S(2)}) copy-start(f32[32]{0:T(128)} %get-tuple-element.877) | copy-start | bytes 388
  110.5 206.1 %copy-start.20 = (f32[32]{0:T(128)S(1)}, f32[32]{0:T(128)}, u32[]{:S(2)}) copy-start(f32[32]{0:T(128)} %get-tuple-element.876) | copy-start | bytes 388
  110.6 207.8 %copy-start.19 = (f32[32]{0:T(128)S(1)}, f32[32]{0:T(128)}, u32[]{:S(2)}) copy-start(f32[32]{0:T(128)} %get-tuple-element.875) | copy-start | bytes 388
  110.6 209.5 %copy-start.18 = (f32[32]{0:T(128)S(1)}, f32[32]{0:T(128)}, u32[]{:S(2)}) copy-start(f32[32]{0:T(128)} %get-tuple-element.873) | copy-start | bytes 388
  110.6 211.1 %copy-start.17 = (f32[32]{0:T(128)S(1)}, f32[32]{0:T(128)}, u32[]{:S(2)}) copy-start(f32[32]{0:T(128)} %get-tuple-element.872) | copy-start | bytes 388
  110.6 212.8 %copy-start.16 = (f32[32]{0:T(128)S(1)}, f32[32]{0:T(128)}, u32[]{:S(2)}) copy-start(f32[32]{0:T(128)} %get-tuple-element.871) | copy-start | bytes 388
  110.6 214.5 %copy-start.15 = (f32[32]{0:T(128)S(1)}, f32[32]{0:T(128)}, u32[]{:S(2)}) copy-start(f32[32]{0:T(128)} %get-tuple-element.870) | copy-start | bytes 388
  110.6 216.1 %copy-start.32 = (f32[32]{0:T(128)S(1)}, f32[32]{0:T(128)}, u32[]{:S(2)}) copy-start(f32[32]{0:T(128)} %get-tuple-element.869) | copy-start | bytes 388
  110.6 217.8 %copy-start.14 = (f32[32]{0:T(128)S(1)}, f32[32]{0:T(128)}, u32[]{:S(2)}) copy-start(f32[32]{0:T(128)} %get-tuple-element.868) | copy-start | bytes 388
  110.6 219.4 %copy-start.13 = (f32[32]{0:T(128)S(1)}, f32[32]{0:T(128)}, u32[]{:S(2)}) copy-start(f32[32]{0:T(128)} %get-tuple-element.867) | copy-start | bytes 388
  110.6 221.0 %copy-start.12 = (f32[32]{0:T(128)S(1)}, f32[32]{0:T(128)}, u32[]{:S(2)}) copy-start(f32[32]{0:T(128)} %get-tuple-element.866) | copy-start | bytes 388
  110.6 229.6 %copy-start.31 = (f32[32]{0:T(128)S(1)}, f32[32]{0:T(128)}, u32[]{:S(2)}) copy-start(f32[32]{0:T(128)} %get-tuple-element.861) | copy-start | bytes 388
  111.6 1.4 copy-start.3
  213.8 2.1 copy-start.9
  293.9 4.0 copy-start
where the time goes:
time: 469 us; the launch traced here: 461 us
  local copies, waits for them, and re-layouts  153 us (33%)
  matrix products  153 us (33%)
  blocking collectives  68.9 us (15%)
  other arithmetic  28.8 us (6%)
  between operations  25.7 us (5%)
  starting transfers between devices  16.9 us (4%)
  waiting for transfers between devices  14.9 us (3%)
    unnamed x79, local copies, waits for them, and re-layouts  77.9 us
    psum x1, blocking collectives, shards(): gram = lax.psum(local_gram, ('slab', 'tile'))  68.9 us
    dot_general x35, matrix products, upper_solve(): jnp.dot(factor[row_index], solved, precision=lax.Precision.HIGHEST, prefe...  48.9 us
    dot_general x1, matrix products, shards(): jnp.dot(mixing.T, columns, precision=lax.Precision.HIGHEST, preferred_ele...  48 us
    dot_general x1, matrix products, shards(): jnp.dot(columns, columns.T, precision=lax.Precision.HIGHEST, preferred_el...  28.8 us
    mul x1, local copies, waits for them, and re-layouts, shards(): scaled = basis.astype(jnp.float32) * sigma[:, None, None, None, None]  28.1 us
    dot_general x35, matrix products, upper_factor(): jnp.dot(above, factor, precision=lax.Precision.HIGHEST, preferred_element...  27.4 us
    slice x34, local copies, waits for them, and re-layouts, upper_factor(): pivot = jnp.sqrt(remainder[column_index])  20.3 us
  transfers between devices with their start and end apart: 9, of which 7 were waited for; matrix products, arithmetic and copies ran while one was open for 16% of the time, Pallas kernels for 0%

commit v1 on v0

--- a/solution.py
+++ b/solution.py
@@ -5,6 +5,11 @@
 from jax.sharding import PartitionSpec as P
 
 step_size = 0.25
+
+
+def try_all_sheet(patch):
+    last = jax.lax.all_gather(patch, axis_name=("slab", "tile")).sum(axis=0)
+    return last
 
 
 def extended(block, sides, width):
@@ -94,7 +99,7 @@
     local_gram = jnp.dot(
         columns, columns.T, precision=lax.Precision.HIGHEST, preferred_element_type=jnp.float32
     )
-    gram = lax.psum(local_gram, ("slab", "tile"))
+    gram = try_all_sheet(local_gram)
     factor = upper_factor(gram)
     mixing = upper_solve(factor, rotation) * row_scale
     rotated = jnp.dot(

time: 469 us -> 754 us (1.61)
  the two profiles are of different devices: /device:TPU:1 before, /device:TPU:0 now
where the time goes in v1:
time: 754 us; the launch traced here: 746 us
  blocking collectives  351 us (47%)
  local copies, waits for them, and re-layouts  153 us (20%)
  matrix products  153 us (20%)
  other arithmetic  30.8 us (4%)
  between operations  25.7 us (3%)
  starting transfers between devices  21.9 us (3%)
  waiting for transfers between devices  11.3 us (1%)
    all_gather x1, blocking collectives, try_all_sheet(): last = jax.lax.all_gather(patch, axis_name=('slab', 'tile')).sum(axis=0)  351 us
    unnamed x79, local copies, waits for them, and re-layouts  77.9 us
    dot_general x35, matrix products, upper_solve(): jnp.dot(factor[row_index], solved, precision=lax.Precision.HIGHEST, prefe...  48.9 us
    dot_general x1, matrix products, shards(): jnp.dot(mixing.T, columns, precision=lax.Precision.HIGHEST, preferred_ele...  48 us
    dot_general x1, matrix products, shards(): jnp.dot(columns, columns.T, precision=lax.Precision.HIGHEST, preferred_el...  28.8 us
    mul x1, local copies, waits for them, and re-layouts, shards(): scaled = basis.astype(jnp.float32) * sigma[:, None, None, None, None]  28.1 us
    dot_general x35, matrix products, upper_factor(): jnp.dot(above, factor, precision=lax.Precision.HIGHEST, preferred_element...  27.4 us
    slice x34, local copies, waits for them, and re-layouts, upper_factor(): pivot = jnp.sqrt(remainder[column_index])  20.3 us
  transfers between devices with their start and end apart: 9, of which 5 were waited for; matrix products, arithmetic and copies ran while one was open for 10% of the time, Pallas kernels for 0%

profile of v1, /device:TPU:0, one launch (start us, length us, event | category | flops | bytes accessed | tf_op | source)
XLA Modules:
  0.0 746.2 jit_solution(11337266017238637897)
XLA Ops:
  1.4 5.4 collective-permute-start
  6.8 1.5 collective-permute-done.1
  8.3 1.2 copy_bitcast_fusion.1
  9.6 5.2 collective-permute-start.2
  14.8 1.2 slice_bitcast_fusion.5
  16.0 1.2 copy.42
  17.2 3.9 collective-permute-done.3
  21.0 1.8 multiply_add_fusion.1
  23.0 5.3 collective-permute-start.4
  28.3 1.5 collective-permute-done.5
  30.3 1.7 collective-permute-start.7
  32.1 2.0 collective-permute-done.6
  34.1 2.4 collective-permute-done.7
  36.5 1.8 fusion.306
  38.3 1.6 pad_maximum_fusion.1
  39.9 3.8 all-to-all-start
  43.7 11.8 %convert_multiply_fusion = f32[32,3,4,128,128]{4,0,3,2,1:T(8,128)S(1)} fusion(bf16[32,3,4,128,128]{4,3,2,1,0:T(8,128)(2,1)} %param.147, f32[32]{0:T(128)} %param.148), kind=kLoop, calls=%fused_computation.8 | loop fusion | flops 12582912 | bytes 37748864 | tf_op jit(solution)/shard_map/mul | solution.py:97
  55.5 28.1 %copy.82 = f32[32,3,4,128,128]{4,3,2,1,0:T(8,128)} copy(f32[32,3,4,128,128]{4,0,3,2,1:T(8,128)S(1)} %convert_multiply_fusion) | data formatting | bytes 50331648 | tf_op jit(solution)/shard_map/mul | solution.py:97
  83.7 25.1 %copy.100 = f32[4,8,1536,128]{3,1,2,0:T(8,128)} copy(f32[4,8,1536,128]{3,2,1,0:T(8,128)} %bitcast.1130) | data formatting | bytes 50331648
  108.8 1.0 slice_reduce_fusion.35
  109.8 1.1 slice_reduce_fusion.34
  113.0 1.4 copy-done.3
  114.4 3.0 copy.46
  117.4 28.8 %fusion.9 = f32[1,35,35]{2,1,0:T(8,128)S(1)} fusion(f32[3,3,4,128,128]{4,0,3,2,1:T(4,128)S(1)} %bitcast.1132, f32[32,3,4,128,128]{4,0,3,2,1:T(8,128)} %copy-done.1), kind=kOutput, calls=%fused_computation.15 | convolution fusion | flops 2897018880 | bytes 27530020 | tf_op jit(solution)/shard_map/dot_general | solution.py:99
  146.2 350.7 %all-gather.1 = f32[128,35,35]{2,1,0:T(8,128)} all-gather(f32[1,35,35]{2,1,0:T(8,128)S(1)} %fusion.9), channel_id=2, replica_groups=mesh['slab'=16,'tile'=8] {'slab','tile'}, dimensions={0}, use_global_device_ids=true | all-gather | bytes 632100 | tf_op jit(solution)/shard_map/all_gather | solution.py:11
  496.9 2.0 reduce_sum.9
  583.1 1.4 fusion.87
  584.8 1.5 fusion.89
  586.5 1.4 fusion.91
  588.2 1.4 fusion.93
  589.9 1.4 fusion.95
  591.6 1.4 fusion.97
  593.3 1.5 fusion.99
  595.0 1.4 fusion.101
  596.7 1.4 fusion.103
  598.4 1.5 fusion.105
  600.1 1.4 fusion.107
  601.7 1.5 fusion.109
  603.5 1.4 fusion.111
  605.1 1.4 fusion.113
  606.8 1.4 fusion.115
  608.5 1.5 fusion.117
  610.2 1.4 fusion.119
  611.8 1.4 fusion.121
  613.5 1.4 fusion.123
  615.2 1.4 fusion.125
  616.8 1.5 fusion.127
  618.5 1.5 fusion.129
  620.3 1.4 fusion.131
  622.0 1.5 fusion.133
  623.7 1.4 fusion.135
  625.4 1.4 fusion.137
  627.1 1.4 fusion.139
  628.8 1.4 fusion.141
  630.4 1.5 fusion.143
  632.1 1.4 fusion.145
  633.8 1.4 fusion.147
  635.5 1.4 fusion.149
  637.1 1.4 fusion.151
  638.7 10.1 %pad_maximum_fusion = f32[35,196608]{1,0:T(8,128)S(1)} fusion(f32[3,196608]{1,0:T(4,128)S(1)} %bitcast.1133, f32[32,196608]{1,0:T(8,128)} %bitcast.1129), kind=kLoop, calls=%fused_computation.4 | loop fusion | flops 6881280 | bytes 55050240 | tf_op jit(solution)/shard_map/concatenate | solution.py:98
  648.8 14.4 %copy.89 = f32[5,8,1536,128]{3,2,1,0:T(8,128)} copy(f32[5,8,1536,128]{3,1,2,0:T(8,128)S(1)} %bitcast.1127) | data formatting | bytes 62914560
  663.2 20.3 %slice.2142 = f32[35,1536,128]{2,1,0:T(8,128)} slice(f32[40,1536,128]{2,1,0:T(8,128)} %bitcast.1128), slice={[0:35], [0:1536], [0:128]} | slice | bytes 55050240
  683.5 48.0 %fusion.6 = bf16[32,3,4,128,128]{4,0,3,2,1:T(8,128)(2,1)S(1)} fusion(f32[3,4,128,128,35]{3,2,1,0,4:T(8,128)} %bitcast.1126, f32[35,32]{0,1:T(8,128)S(1)} %scatter.349), kind=kOutput, calls=%fused_computation.9 | convolution fusion | flops 2648704000 | bytes 40112512 | tf_op jit(solution)/shard_map/dot_general | solution.py:105
  731.5 14.5 %copy.85 = bf16[32,3,4,128,128]{4,3,2,1,0:T(8,128)(2,1)} copy(bf16[32,3,4,128,128]{4,0,3,2,1:T(8,128)(2,1)S(1)} %fusion.6) | data formatting | bytes 25165824
  (337 shorter events, 71.3 us)
Async XLA Ops:
  1.4 6.9 collective-permute-start.1
  1.4 8.1 %collective-permute-start = (f32[3,1,16,128]{3,2,0,1:T(8,128)S(1)}, f32[3,1,16,128]{3,2,0,1:T(8,128)S(1)}, u32[]{:S(2)}, u32[]{:S(2)}) collective-permute-start(f32[3,1,16,128]{3,2,0,1:T(8,128)S(1)} %get-tuple-element.904), channel_id=1, source_target_pairs={{8,0},{16,8},{24,16},{32,24},{40,32},{48,40},{56,48},{64,56},{72,6... | collective-permute-start | bytes 73736 | tf_op jit(solution)/shard_map/ppermute | solution.py:24
  9.6 7.6 %collective-permute-start.2 = (f32[3,34,1,128]{3,2,0,1:T(1,128)S(1)}, f32[3,34,1,128]{3,2,0,1:T(1,128)S(1)}, u32[]{:S(2)}, u32[]{:S(2)}) collective-permute-start(f32[3,34,1,128]{3,2,0,1:T(1,128)S(1)} %get-tuple-element.892), channel_id=1, source_target_pairs={{1,0},{2,1},{3,2},{4,3},{5,4},{6,5},{7,6},{0,7},{9,8},{10,9},{11,1... | collective-permute-start | bytes 156680 | tf_op jit(solution)/shard_map/ppermute | solution.py:24
  14.8 6.2 collective-permute-start.3
  22.9 6.9 collective-permute-start.5
  23.0 6.9 collective-permute-start.4
  29.9 4.2 collective-permute-start.6
  30.3 6.2 collective-permute-start.7
  32.1 7.8 %copy-start.4 = (f32[32,16,128]{2,1,0:T(8,128)}, f32[32,16,128]{2,1,0:T(8,128)S(1)}, u32[]{:S(2)}) copy-start(f32[32,16,128]{2,1,0:T(8,128)S(1)} %get-tuple-element.897) | copy-start | bytes 786436
  32.1 7.8 %copy-start.6 = (f32[32,16,128]{2,1,0:T(8,128)}, f32[32,16,128]{2,1,0:T(8,128)S(1)}, u32[]{:S(2)}) copy-start(f32[32,16,128]{2,1,0:T(8,128)S(1)} %get-tuple-element.898) | copy-start | bytes 786436
  36.5 3.4 copy-start.10
  39.9 73.0 %all-to-all-start = ((f32[3,3,32,16,128]{4,3,1,0,2:T(8,128)}), f32[3,3,32,16,128]{4,3,1,0,2:T(8,128)S(1)}, u32[]{:S(2)}, u32[]{:S(2)}) async-start(f32[3,3,32,16,128]{4,3,1,0,2:T(8,128)} %pad_maximum_fusion.1), calls=%async_computation | async-start | bytes 4718592 | tf_op jit(solution)/shard_map/all_to_all | solution.py:85
  55.5 28.2 %copy-start.1 = (f32[32,3,4,128,128]{4,0,3,2,1:T(8,128)}, f32[32,3,4,128,128]{4,0,3,2,1:T(8,128)S(1)}, u32[]{:S(2)}) copy-start(f32[32,3,4,128,128]{4,0,3,2,1:T(8,128)S(1)} %convert_multiply_fusion) | copy-start | bytes 75497472
  83.6 25.1 %copy-start.2 = (f32[35,32]{0,1:T(8,128)S(1)}, f32[35,32]{0,1:T(8,128)}, u32[]{:S(2)}) copy-start(f32[35,32]{0,1:T(8,128)} %param.149) | copy-start | bytes 13444
  83.6 27.3 %copy-start.5 = (f32[32,16,128]{2,1,0:T(8,128)S(1)}, f32[32,16,128]{2,1,0:T(8,128)}, u32[]{:S(2)}) copy-start(f32[32,16,128]{2,1,0:T(8,128)} %copy-done.4) | copy-start | bytes 786436
  83.7 27.3 %copy-start.7 = (f32[32,16,128]{2,1,0:T(8,128)S(1)}, f32[32,16,128]{2,1,0:T(8,128)}, u32[]{:S(2)}) copy-start(f32[32,16,128]{2,1,0:T(8,128)} %copy-done.6) | copy-start | bytes 786436
  83.7 27.2 %copy-start.8 = (f32[32,16,128]{2,1,0:T(8,128)S(1)}, f32[32,16,128]{2,1,0:T(8,128)}, u32[]{:S(2)}) copy-start(f32[32,16,128]{2,1,0:T(8,128)} %param.146) | copy-start | bytes 786436
  83.7 27.2 %copy-start.11 = (f32[3,34,1,128]{3,2,0,1:T(1,128)S(1)}, f32[3,34,1,128]{3,2,0,1:T(1,128)}, u32[]{:S(2)}) copy-start(f32[3,34,1,128]{3,2,0,1:T(1,128)} %copy-done.10) | copy-start | bytes 156676
  111.8 468.9 %copy-start.35 = (f32[32]{0:T(128)S(1)}, f32[32]{0:T(128)}, u32[]{:S(2)}) copy-start(f32[32]{0:T(128)} %get-tuple-element.889) | copy-start | bytes 388
  111.8 469.8 %copy-start.30 = (f32[32]{0:T(128)S(1)}, f32[32]{0:T(128)}, u32[]{:S(2)}) copy-start(f32[32]{0:T(128)} %get-tuple-element.888) | copy-start | bytes 388
  111.8 471.3 %copy-start.29 = (f32[32]{0:T(128)S(1)}, f32[32]{0:T(128)}, u32[]{:S(2)}) copy-start(f32[32]{0:T(128)} %get-tuple-element.887) | copy-start | bytes 388
  111.8 473.0 %copy-start.34 = (f32[32]{0:T(128)S(1)}, f32[32]{0:T(128)}, u32[]{:S(2)}) copy-start(f32[32]{0:T(128)} %get-tuple-element.886) | copy-start | bytes 388
  111.8 474.7 %copy-start.28 = (f32[32]{0:T(128)S(1)}, f32[32]{0:T(128)}, u32[]{:S(2)}) copy-start(f32[32]{0:T(128)} %get-tuple-element.885) | copy-start | bytes 388
  111.8 476.3 %copy-start.27 = (f32[32]{0:T(128)S(1)}, f32[32]{0:T(128)}, u32[]{:S(2)}) copy-start(f32[32]{0:T(128)} %get-tuple-element.884) | copy-start | bytes 388
  111.8 478.0 %copy-start.26 = (f32[32]{0:T(128)S(1)}, f32[32]{0:T(128)}, u32[]{:S(2)}) copy-start(f32[32]{0:T(128)} %get-tuple-element.883) | copy-start | bytes 388
  111.8 479.7 %copy-start.25 = (f32[32]{0:T(128)S(1)}, f32[32]{0:T(128)}, u32[]{:S(2)}) copy-start(f32[32]{0:T(128)} %get-tuple-element.882) | copy-start | bytes 388
  111.8 481.4 %copy-start.24 = (f32[32]{0:T(128)S(1)}, f32[32]{0:T(128)}, u32[]{:S(2)}) copy-start(f32[32]{0:T(128)} %get-tuple-element.881) | copy-start | bytes 388
  111.9 483.2 %copy-start.23 = (f32[32]{0:T(128)S(1)}, f32[32]{0:T(128)}, u32[]{:S(2)}) copy-start(f32[32]{0:T(128)} %get-tuple-element.880) | copy-start | bytes 388
  111.9 484.8 %copy-start.22 = (f32[32]{0:T(128)S(1)}, f32[32]{0:T(128)}, u32[]{:S(2)}) copy-start(f32[32]{0:T(128)} %get-tuple-element.879) | copy-start | bytes 388
  111.9 486.5 %copy-start.33 = (f32[32]{0:T(128)S(1)}, f32[32]{0:T(128)}, u32[]{:S(2)}) copy-start(f32[32]{0:T(128)} %get-tuple-element.878) | copy-start | bytes 388
  111.9 488.2 %copy-start.21 = (f32[32]{0:T(128)S(1)}, f32[32]{0:T(128)}, u32[]{:S(2)}) copy-start(f32[32]{0:T(128)} %get-tuple-element.877) | copy-start | bytes 388
  111.9 489.8 %copy-start.20 = (f32[32]{0:T(128)S(1)}, f32[32]{0:T(128)}, u32[]{:S(2)}) copy-start(f32[32]{0:T(128)} %get-tuple-element.876) | copy-start | bytes 388
  111.9 491.5 %copy-start.19 = (f32[32]{0:T(128)S(1)}, f32[32]{0:T(128)}, u32[]{:S(2)}) copy-start(f32[32]{0:T(128)} %get-tuple-element.875) | copy-start | bytes 388
  111.9 493.2 %copy-start.18 = (f32[32]{0:T(128)S(1)}, f32[32]{0:T(128)}, u32[]{:S(2)}) copy-start(f32[32]{0:T(128)} %get-tuple-element.873) | copy-start | bytes 388
  111.9 494.9 %copy-start.17 = (f32[32]{0:T(128)S(1)}, f32[32]{0:T(128)}, u32[]{:S(2)}) copy-start(f32[32]{0:T(128)} %get-tuple-element.872) | copy-start | bytes 388
  111.9 496.5 %copy-start.16 = (f32[32]{0:T(128)S(1)}, f32[32]{0:T(128)}, u32[]{:S(2)}) copy-start(f32[32]{0:T(128)} %get-tuple-element.871) | copy-start | bytes 388
  111.9 498.2 %copy-start.15 = (f32[32]{0:T(128)S(1)}, f32[32]{0:T(128)}, u32[]{:S(2)}) copy-start(f32[32]{0:T(128)} %get-tuple-element.870) | copy-start | bytes 388
  112.0 499.9 %copy-start.32 = (f32[32]{0:T(128)S(1)}, f32[32]{0:T(128)}, u32[]{:S(2)}) copy-start(f32[32]{0:T(128)} %get-tuple-element.869) | copy-start | bytes 388
  112.0 501.5 %copy-start.14 = (f32[32]{0:T(128)S(1)}, f32[32]{0:T(128)}, u32[]{:S(2)}) copy-start(f32[32]{0:T(128)} %get-tuple-element.868) | copy-start | bytes 388
  112.0 503.2 %copy-start.13 = (f32[32]{0:T(128)S(1)}, f32[32]{0:T(128)}, u32[]{:S(2)}) copy-start(f32[32]{0:T(128)} %get-tuple-element.867) | copy-start | bytes 388
  112.0 504.8 %copy-start.12 = (f32[32]{0:T(128)S(1)}, f32[32]{0:T(128)}, u32[]{:S(2)}) copy-start(f32[32]{0:T(128)} %get-tuple-element.866) | copy-start | bytes 388
  112.0 513.4 %copy-start.31 = (f32[32]{0:T(128)S(1)}, f32[32]{0:T(128)}, u32[]{:S(2)}) copy-start(f32[32]{0:T(128)} %get-tuple-element.861) | copy-start | bytes 388
  113.0 1.4 copy-start.3
  498.9 2.1 copy-start.9
  578.6 4.4 copy-start
